TPU v7x, 256 devices: a whole 4x4x8 slice. The times are simulated.
256 devices in a mesh: tm: 64 (over z, x, core), head: 4 (over y).
Axes of the slice: x: 4, y: 4, z: 8, core: 2. Of those that a mesh axis runs over, the one named last changes fastest.
Arguments:
- frames: bfloat16 [65536, 1024], P('tm'), may hold values from -6 to 6
- grad_out: bfloat16 [65536, 1024], P('tm', 'head'), may hold values from -6 to 6
- w_query: bfloat16 [1024, 1024], P(None, 'head'), may hold values from -0.1875 to 0.1875
- w_key: bfloat16 [1024, 1024], P(None, 'head'), may hold values from -0.1875 to 0.1875
- w_value: bfloat16 [1024, 1024], P(None, 'head'), may hold values from -0.1875 to 0.1875
Outputs:
- grad_input: bfloat16 [65536, 1024], P('tm', 'head')
- grad_wq: float32 [1024, 1024], P('tm', 'head')
- grad_wk: float32 [1024, 1024], P('tm', 'head')
- grad_wv: float32 [1024, 1024], P('tm', 'head')
All inputs are finite; a program needn't handle non-finite values.
Results may differ from a plain program's by a relative error of at most 0.0095.
Values may be sent and summed in bfloat16 or wider, within the bound.
A program may use at most 64 MiB of HBM per device.

v0:
```python
import jax
import jax.numpy as jnp
from jax import lax
from jax.sharding import PartitionSpec as P

DH = 64


def entering(part, axis, combine, identity, reverse):
    count = lax.axis_size(axis)
    place = lax.axis_index(axis)
    ahead = count - 1 - place if reverse else place
    gathered = lax.all_gather(part, axis)
    state = jnp.zeros_like(part) + jnp.asarray(identity, part.dtype)

    def one(turn, state):
        source = count - 1 - turn if reverse else turn
        return combine(state, lax.dynamic_index_in_dim(gathered, source, 0, False))

    return lax.fori_loop(0, ahead, one, state)


def contract_first(left, right):
    return lax.dot_general(
        left, right, (((0,), (0,)), ((), ())), preferred_element_type=jnp.float32
    )


def contract_last(left, right):
    return lax.dot_general(
        left, right, (((1,), (1,)), ((), ())), preferred_element_type=jnp.float32
    )


def exact_dot(left, right):
    return jnp.dot(left, right, precision=lax.Precision.HIGHEST)


def add_states(earlier, later):
    return earlier + later


def local(frames, grad_out, w_query, w_key, w_value):
    frame_rows = frames.shape[0]
    group_width = w_query.shape[1]
    heads_local = group_width // DH
    time_devices = lax.axis_size("tm")
    scale_factor = float(DH * frame_rows * time_devices) ** (-0.5)
    weights_joined = jnp.concatenate((w_query, w_key, w_value), axis=1)
    projected = jnp.dot(frames, weights_joined, preferred_element_type=jnp.float32).astype(
        jnp.bfloat16
    )

    def head_first(array):
        return array.reshape(frame_rows, heads_local, DH).transpose(1, 0, 2)

    query_heads = head_first(projected[:, :group_width])
    key_heads = head_first(projected[:, group_width : 2 * group_width])
    value_heads = head_first(projected[:, 2 * group_width :])
    grad_heads = head_first(grad_out)
    key_value = jnp.einsum(
        "hti,htj->hij",
        key_heads.astype(jnp.float32),
        value_heads.astype(jnp.float32),
        precision=lax.Precision.HIGHEST,
    )
    query_grad = jnp.einsum(
        "hti,htj->hij",
        query_heads.astype(jnp.float32),
        grad_heads.astype(jnp.float32),
        precision=lax.Precision.HIGHEST,
    )
    zero_state = jnp.zeros_like(key_value)
    prefix = entering(key_value, "tm", add_states, zero_state, False)
    suffix = entering(query_grad, "tm", add_states, zero_state, True)
    causal = jnp.arange(frame_rows)[:, None] >= jnp.arange(frame_rows)[None, :]

    def one_head(items):
        query_rows, key_rows, value_rows, grad_rows, prefix_state, suffix_state = items
        grad_scores = jnp.where(causal, contract_last(grad_rows, value_rows), 0.0).astype(
            jnp.bfloat16
        )
        key_scores = jnp.where(causal, contract_last(query_rows, key_rows), 0.0).astype(
            jnp.bfloat16
        )
        grad32 = grad_rows.astype(jnp.float32)
        value32 = value_rows.astype(jnp.float32)
        key32 = key_rows.astype(jnp.float32)
        dquery = jnp.dot(grad_scores, key_rows, preferred_element_type=jnp.float32) + exact_dot(
            grad32, prefix_state.T
        )
        dkey = contract_first(grad_scores, query_rows) + exact_dot(value32, suffix_state.T)
        dvalue = contract_first(key_scores, grad_rows) + exact_dot(key32, suffix_state)
        return (
            (dquery * scale_factor).astype(jnp.bfloat16),
            (dkey * scale_factor).astype(jnp.bfloat16),
            (dvalue * scale_factor).astype(jnp.bfloat16),
        )

    dquery, dkey, dvalue = lax.map(
        one_head, (query_heads, key_heads, value_heads, grad_heads, prefix, suffix)
    )

    def rows_first(array):
        return array.transpose(1, 0, 2).reshape(frame_rows, group_width)

    grads_joined = jnp.concatenate(
        (rows_first(dquery), rows_first(dkey), rows_first(dvalue)), axis=1
    )
    input_part = contract_last(grads_joined, weights_joined).astype(jnp.bfloat16)
    input_part = lax.optimization_barrier(input_part).astype(jnp.float32)
    grad_input = lax.psum_scatter(
        input_part.astype(jnp.bfloat16), "head", scatter_dimension=1, tiled=True
    )
    weight_terms = contract_first(frames, grads_joined)
    weight_share = lax.psum_scatter(weight_terms, "tm", scatter_dimension=0, tiled=True)
    grad_wq = weight_share[:, :group_width]
    grad_wk = weight_share[:, group_width : 2 * group_width]
    grad_wv = weight_share[:, 2 * group_width :]
    return (grad_input, grad_wq, grad_wk, grad_wv)


def solution(mesh):
    placed = (P("tm", None), P("tm", "head"), P(None, "head"), P(None, "head"), P(None, "head"))
    return jax.shard_map(
        local,
        mesh=mesh,
        in_specs=placed,
        out_specs=(P("tm", "head"), P("tm", "head"), P("tm", "head"), P("tm", "head")),
        check_vma=False,
    )
```

profile of v0, /device:TPU:1, one launch (start us, length us, event | category | flops | bytes accessed | tf_op | source)
XLA Modules:
  0.0 472.2 jit_solution(10810908242285416440)
XLA Ops:
  9.7 1.9 fusion.62
  12.7 2.0 fusion.67
  15.8 2.1 fusion.68
  18.0 84.0 %all-gather.5.cloned.1.call-done = f32[256,64,64]{2,1,0:T(8,128)} async-done(((f32[4,64,64]{2,1,0:T(8,128)}), f32[256,64,64]{2,1,0:T(8,128)}) %all-gather.5.cloned.1.call-update) | async-done | bytes 4194320 | tf_op jit(solution)/shard_map/all_gather | solution.py:13
  103.0 81.6 %all-gather.7.cloned.1.call-done = f32[256,64,64]{2,1,0:T(8,128)} async-done(((f32[4,64,64]{2,1,0:T(8,128)}), f32[256,64,64]{2,1,0:T(8,128)}) %all-gather.7.cloned.1.call-update) | async-done | bytes 4194320 | tf_op jit(solution)/shard_map/all_gather | solution.py:13
  184.5 59.9 %while.39 = (s32[]{:T(128)}, f32[4,64,64]{2,1,0:T(8,128)S(1)}, s32[]{:T(128)}, f32[64,4,64,64]{3,2,1,0:T(8,128)}, s32[]{:T(128)}, /*index=5*/s32[]{:T(128)}, s32[]{:T(128)}, s32[]{:T(128)}) while((s32[]{:T(128)}, f32[4,64,64]{2,1,0:T(8,128)S(1)}, s32[]{:T(128)}, f32[64,4,64,64]{3,2,1,0:T(8,128)}, s32[]{:T(128)}, /*index=5*/s32[]{:T(128)}, ...), condition=%wide.region_3.4_spmd, body=%wide.region_2.3_spmd.sunk | while | flops 16390 | bytes 196743 | solution.py:20
  244.5 41.9 %while.40 = (s32[]{:T(128)}, bf16[4,1024,64]{1,2,0:T(8,128)(2,1)}, bf16[4,1024,64]{1,2,0:T(8,128)(2,1)}, bf16[4,1024,64]{1,2,0:T(8,128)(2,1)}, bf16[4,1024,64]{1...) while((s32[]{:T(128)}, bf16[4,1024,64]{1,2,0:T(8,128)(2,1)}, ...), condition=%wide.region_5.6_spmd.clone.clone, body=%wide.region_4.5_spmd.clone.clone.sunk | while | flops 828964864 | bytes 9674353 | solution.py:100
  247.0 1.8 fusion.118
  250.0 2.1 fusion.120
  252.4 2.6 fusion.122
  257.5 1.8 fusion.118
  260.5 2.1 fusion.120
  262.8 2.6 fusion.122
  268.0 1.8 fusion.118
  271.0 2.1 fusion.120
  273.3 2.6 fusion.122
  278.5 1.8 fusion.118
  281.4 2.1 fusion.120
  283.8 2.6 fusion.122
  286.4 4.8 %convolution_bitcast_fusion = f32[1024,768]{0,1:T(8,128)} fusion(bf16[1024,1024]{1,0:T(8,128)(2,1)S(1)} %copy-done, bf16[1024,256]{0,1:T(8,128)(2,1)} %bitcast.142, bf16[1024,256]{0,1:T(8,128)(2,1)} %bitcast.20, bf16[1024,256]{0,1:T(8,128)(2,1)} %bitcast.18), kind=kOutput, calls=%fused_computation.61 | convolution fusion | flops 1615331328 | bytes 6815744 | tf_op jit(solution)/shard_map/dot_general | solution.py:24
  291.3 3.5 copy.32
  295.8 4.9 %convolution_convert_fusion = bf16[1024,1024]{1,0:T(8,128)(2,1)} fusion(bf16[1024,768]{1,0:T(8,128)(2,1)} %copy-done.3, bf16[1024,256]{0,1:T(8,128)(2,1)S(1)} %bitcast.143, bf16[1024,256]{0,1:T(8,128)(2,1)} %bitcast.20, bf16[1024,256]{0,1:T(8,128)(2,1)} %bitcast.18), kind=kOutput, calls=%fused_computation.62 | convolution fusion | flops 1616379904 | bytes 5242880 | tf_op jit(solution)/shard_map/dot_general | solution.py:30
  300.8 126.1 %reduce-scatter.7.cloned.1.call-done = f32[16,768]{1,0:T(8,128)} async-done(((f32[1024,768]{1,0:T(8,128)}), f32[16,768]{1,0:T(8,128)}) %reduce-scatter.7.cloned.1.call-update) | async-done | bytes 49168
  428.2 37.5 %reduce-scatter.5.cloned.1.call-done = bf16[1024,256]{1,0:T(8,128)(2,1)} async-done(((bf16[1024,1024]{1,0:T(8,128)(2,1)}), bf16[1024,256]{1,0:T(8,128)(2,1)}) %reduce-scatter.5.cloned.1.call-update) | async-done | bytes 524304 | tf_op jit(solution)/shard_map/reduce_scatter | solution.py:112
  (109 shorter events, 83.2 us)
Async XLA Ops:
  7.2 2.5 copy-start
  7.2 2.4 copy-start.1
  7.2 94.8 %all-gather.5.cloned.1.call-start = ((), (), s32[]{:S(2)}) async-start(), calls=%async_computation.3 | async-start | bytes 8519680 | tf_op jit(solution)/shard_map/all_gather | solution.py:13
  9.6 1.9 copy-start.3
  11.5 3.2 copy-start.2
  14.7 169.9 %all-gather.7.cloned.1.call-start = ((), (), s32[]{:S(2)}) async-start(), calls=%async_computation.4 | async-start | bytes 8519680 | tf_op jit(solution)/shard_map/all_gather | solution.py:13
  17.9 409.0 %reduce-scatter.7.cloned.1.call-start = ((), (), s32[]{:S(2)}) async-start(), calls=%async_computation.5 | async-start | bytes 3194880
  294.8 1.0 copy-start.4
  294.8 170.9 %reduce-scatter.5.cloned.1.call-start = ((), (), s32[]{:S(2)}) async-start(), calls=%async_computation.2 | async-start | bytes 2621440 | tf_op jit(solution)/shard_map/reduce_scatter | solution.py:112
Sparse Core Ops, SparseCore 0:
  14.8 87.1 all-gather.4
  104.7 79.7 all-gather.6
  294.9 131.8 reduce-scatter.6
  429.8 35.8 reduce-scatter.4
where the time goes:
time: 474 us; the launch traced here: 472 us
  waiting for transfers between devices  329 us (69%)
  other arithmetic  59.2 us (12%)
  matrix products  57.6 us (12%)
  between operations  13.9 us (3%)
  local copies, waits for them, and re-layouts  10.5 us (2%)
    all_gather x2, waiting for transfers between devices, entering(): gathered = lax.all_gather(part, axis)  166 us
    unnamed x5, waiting for transfers between devices  126 us
    add x63, other arithmetic, add_states(): return earlier + later  59.2 us
    reduce_scatter x1, waiting for transfers between devices, local(): lax.psum_scatter(input_part.astype(jnp.bfloat16), 'head', scatter_dimensi...  37.5 us
    dot_general x9, matrix products, contract_first(): lax.dot_general(left, right, (((0,), (0,)), ((), ())), preferred_element_...  23.5 us
    dot_general x12, matrix products, exact_dot(): return jnp.dot(left, right, precision=lax.Precision.HIGHEST)  13.1 us
    dot_general x5, matrix products, contract_last(): lax.dot_general(left, right, (((1,), (1,)), ((), ())), preferred_element_...  11.9 us
  transfers between devices with their start and end apart: 4, of which 4 were waited for; matrix products, arithmetic and copies ran while one was open for 2% of the time, Pallas kernels for 0%

commit v1 on v0

v1 whole, which is shorter than its diff:
```python
import functools

import jax
import jax.numpy as jnp
from jax import lax
from jax.experimental import pallas as pl
from jax.experimental.pallas import tpu as pltpu
from jax.sharding import PartitionSpec as P

DH = 64
CHUNK = 256
NX = 4
NC = 2
MESH = pl.DeviceIdType.MESH
BF = jnp.bfloat16
F32 = jnp.float32


def nn(a, b):
    return lax.dot_general(a, b, (((1,), (0,)), ((), ())), preferred_element_type=F32)


def nt(a, b):
    return lax.dot_general(a, b, (((1,), (1,)), ((), ())), preferred_element_type=F32)


def tn(a, b):
    return lax.dot_general(a, b, (((0,), (0,)), ((), ())), preferred_element_type=F32)


def split(value):
    high = value.astype(BF)
    return high, (value - high.astype(F32)).astype(BF)


def kernel(
    dims,
    frames_hbm, grad_hbm, wq_hbm, wk_hbm, wv_hbm,
    gi_ref, gwq_ref, gwk_ref, gwv_ref,
    fr, g_tok, w_all, q_tok, qt, kt, vt, gt, frt,
    kvc, qgc, st, stb, sc_r1, sc_k, sc_zr, sc_acc, sc_p, sc_xr, sc_e, sc_r4, fin,
    d_in, d_t, parts, y_r1, y_r2,
    wg, c_r, w_s1, x_r1, x_r2, w_s2, w_s2f, z_r,
    in_sem, sc_s, sc_rs, zs_s, zs_r, xs_s, xs_r,
    y_s, y_r, c_s, c_rs, w_s, w_r, wz_s, wz_r,
):
    T, D, G, C, NZ, NY, NH, dh = (
        dims[k] for k in ("T", "D", "G", "C", "NZ", "NY", "NH", "DH")
    )
    NCH = T // C
    NM = NZ * NX * NC
    scale = float(dh * T * NM) ** (-0.5)
    R = D // NM
    DB = D // NY

    me = lax.axis_index("tm")
    y = lax.axis_index("head")
    c = lax.rem(me, NC)
    x = lax.rem(lax.div(me, NC), NX)
    z = lax.div(me, NC * NX)

    def at(zz, xx, cc, yy=None):
        return (zz * (NX * NC) + xx * NC + cc, y if yy is None else yy)

    sib = at(z, x, 1 - c)

    copies_in = [
        pltpu.make_async_copy(
            frames_hbm.at[pl.ds(i * C, C), :], fr.at[pl.ds(i * C, C), :], in_sem.at[4 + i]
        )
        for i in range(NCH)
    ]
    copies_w = [
        pltpu.make_async_copy(ref, w_all.at[:, pl.ds(i * G, G)], in_sem.at[i])
        for i, ref in enumerate((wq_hbm, wk_hbm, wv_hbm))
    ]
    copy_g = pltpu.make_async_copy(grad_hbm, g_tok, in_sem.at[3])
    copies_w[1].start()
    copies_in[0].start()
    copies_w[2].start()
    copies_w[0].start()
    copy_g.start()
    for i in range(1, NCH):
        copies_in[i].start()

    barrier = pltpu.get_barrier_semaphore()
    peers = [sib]
    peers += [at(lax.rem(z + d, NZ), x, c) for d in range(1, NZ)]
    peers += [at(z, lax.rem(x + d, NX), c) for d in range(1, NX)]
    y_next, y_prev, y_far = (lax.rem(y + d, NY) for d in (1, NY - 1, 2))
    peers += [(me, y_next), (me, y_prev)]
    for peer in peers:
        pl.semaphore_signal(barrier, inc=1, device_id=peer, device_id_type=MESH)

    row = lax.broadcasted_iota(jnp.int32, (G, G), 0)
    col = lax.broadcasted_iota(jnp.int32, (G, G), 1)
    same = lax.div(row, dh) == lax.div(col, dh)

    def spread(packed):
        return jnp.where(same, jnp.concatenate([packed] * NH, axis=0), 0.0)

    def pack(full):
        total = full[0:dh]
        for h in range(1, NH):
            total = total + full[h * dh : (h + 1) * dh]
        return total

    copies_w[0].wait()
    copies_w[1].wait()
    copies_w[2].wait()
    copy_g.wait()
    for i in range(NCH):
        copies_in[i].wait()

    def project(i, carry):
        here = pl.ds(pl.multiple_of(i * C, C), C)
        f = fr[here, :]
        k = nn(f, w_all[:, G : 2 * G]).astype(BF).T
        v = nn(f, w_all[:, 2 * G :]).astype(BF).T
        kt[:, here] = k
        vt[:, here] = v
        kvc[i] = jnp.where(same, nt(k, v), 0.0)
        q = nn(f, w_all[:, :G]).astype(BF)
        q_tok[here, :] = q
        qf = q.T
        qt[:, here] = qf
        g = g_tok[here, :]
        gt[:, here] = g.T
        qgc[i] = jnp.where(same, nn(qf, g), 0.0)
        return carry

    lax.fori_loop(0, NCH, project, 0)

    st[0] = pack(sum(kvc[i] for i in range(NCH)))
    st[1] = pack(sum(qgc[i] for i in range(NCH)))
    stb[...] = st[...].astype(BF)
    pl.semaphore_wait(barrier, len(peers))

    def remote(src, dst, send, recv, dev):
        return pltpu.make_async_remote_copy(
            src_ref=src, dst_ref=dst, send_sem=send, recv_sem=recv,
            device_id=dev, device_id_type=MESH,
        )

    scan1 = remote(stb.at[1 - c], sc_r1, sc_s.at[0], sc_rs.at[0], sib)
    scan1.start()

    side = 1 - 2 * c
    zp = z + c * (NZ - 1 - 2 * z)
    xp = x + c * (NX - 1 - 2 * x)

    def z_copy(d):
        return remote(
            sc_k, sc_zr.at[d - 1], zs_s.at[d - 1], zs_r.at[d - 1],
            at(lax.rem(z + side * d + NZ, NZ), x, c),
        )

    def scan_z_start():
        scan1.wait()
        sc_k[...] = (st[c] + sc_r1[...].astype(F32)).astype(BF)
        for d in range(1, NZ):
            @pl.when(zp + d < NZ)
            def _():
                z_copy(d).start()

    def x_copy(d, src):
        return remote(
            src, sc_xr.at[d - 1], xs_s.at[d - 1], xs_r.at[d - 1],
            at(z, lax.rem(x + d, NX), c),
        )

    def scan_x_start():
        sc_acc[...] = jnp.zeros_like(sc_acc)
        for d in range(1, NZ):
            @pl.when(zp + d < NZ)
            def _():
                z_copy(d).wait_send()

            @pl.when(zp >= d)
            def _():
                z_copy(d).wait_recv()
                sc_acc[...] += sc_zr[d - 1].astype(F32)
        own = sc_acc[...]
        sc_p[0] = own.astype(BF)
        sc_p[1] = (own + st[c] + sc_r1[...].astype(F32)).astype(BF)
        for d in range(1, NX):
            xt = lax.rem(x + d, NX)
            later = jnp.where(side * (xt - x) > 0, 1, 0)
            x_copy(d, sc_p.at[later]).start()

    scan4 = remote(sc_e, sc_r4, sc_s.at[1], sc_rs.at[1], sib)

    def scan_core_start():
        for d in range(1, NX):
            xt = lax.rem(x + d, NX)
            later = jnp.where(side * (xt - x) > 0, 1, 0)
            x_copy(d, sc_p.at[later]).wait()
        own = sc_acc[...]
        for d in range(1, NX):
            own = own + sc_xr[d - 1].astype(F32)
        fin[c] = own
        sc_e[...] = (own + st[c]).astype(BF)
        scan4.start()

    def scan_end():
        scan4.wait()
        fin[1 - c] = sc_r4[...].astype(F32)

    tri = lax.broadcasted_iota(jnp.int32, (C, C), 0) >= lax.broadcasted_iota(
        jnp.int32, (C, C), 1
    )
    lane_head = lax.div(lax.broadcasted_iota(jnp.int32, (C, G), 1), dh)

    def intra(i):
        here = pl.ds(i * C, C)
        g = g_tok[here, :]
        q = q_tok[here, :]
        kf, vf, qf, gf = kt[:, here], vt[:, here], qt[:, here], gt[:, here]
        zero = jnp.zeros_like(g)
        for h in range(NH):
            rows = slice(h * dh, (h + 1) * dh)
            pg = nn(jnp.where(lane_head == h, g, zero), vf)
            pg = jnp.where(tri, pg, 0.0).astype(BF)
            sk = nn(jnp.where(lane_head == h, q, zero), kf)
            sk = jnp.where(tri, sk, 0.0).astype(BF)
            d_in[pl.ds(h * dh, dh), here] = nt(kf[rows], pg)
            d_in[pl.ds(G + h * dh, dh), here] = nn(qf[rows], pg)
            d_in[pl.ds(2 * G + h * dh, dh), here] = nn(gf[rows], sk)

    def flip(i):
        here = pl.ds(i * C, C)
        for b in range(D // C):
            frt[pl.ds(b * C, C), here] = fr[here, pl.ds(b * C, C)].T

    intra(0)
    scan_z_start()
    intra(1)
    flip(0)
    intra(2)
    flip(1)
    scan_x_start()
    intra(3)
    flip(2)
    scan_core_start()
    flip(3)
    scan_end()

    def finish(i):
        here = pl.ds(i * C, C)
        prefix = spread(fin[0])
        suffix = spread(fin[1])
        for j in range(i):
            prefix = prefix + kvc[j]
        for j in range(i + 1, NCH):
            suffix = suffix + qgc[j]
        ph, pe = split(prefix)
        sh, se = split(suffix)
        kf, vf, gf = kt[:, here], vt[:, here], gt[:, here]
        dq = d_in[pl.ds(0, G), here] + nn(ph, gf) + nn(pe, gf)
        dk = d_in[pl.ds(G, G), here] + nn(sh, vf) + nn(se, vf)
        dv = d_in[pl.ds(2 * G, G), here] + tn(sh, kf) + tn(se, kf)
        d_t[pl.ds(0, G), here] = (dq * scale).astype(BF)
        d_t[pl.ds(G, G), here] = (dk * scale).astype(BF)
        d_t[pl.ds(2 * G, G), here] = (dv * scale).astype(BF)

    HB = DB // 2

    def part(i):
        here = pl.ds(i * C, C)
        grads = d_t[:, here]
        for d in (2, 1, NY - 1, 0):
            b = lax.rem(y + d, NY)
            rows = pl.ds(pl.multiple_of(b * DB, DB), DB)
            value = nn(w_all[rows, :], grads).astype(BF)
            parts[i, b] = value.reshape(2, HB, C)
            if d == 2:
                y_copy(i, 0).start()
                y_copy(i, 1).start()
            if d == 1:
                y_copy(i, 2).start()
            if d == NY - 1:
                y_copy(i, 3).start()

    def y_copy(i, n):
        src, dst, dev = (
            (parts.at[i, y_far, 0], y_r1.at[i, 0], y_next),
            (parts.at[i, y_far, 1], y_r1.at[i, 1], y_prev),
            (parts.at[i, y_next, 1], y_r2.at[i, 0, 1], y_next),
            (parts.at[i, y_prev, 0], y_r2.at[i, 1, 0], y_prev),
            (parts.at[i, y_next, 0], y_r2.at[i, 0, 0], y_next),
            (parts.at[i, y_prev, 1], y_r2.at[i, 1, 1], y_prev),
        )[n]
        return remote(src, dst, y_s.at[i, n], y_r.at[i, n], (me, dev))

    def y_relay(i):
        for n, dest, half in ((0, y_next, 0), (1, y_prev, 1)):
            y_copy(i, n).wait()
            parts[i, dest, half] = (
                parts[i, dest, half].astype(F32) + y_r1[i, half].astype(F32)
            ).astype(BF)
            y_copy(i, 4 + n).start()

    def y_final(i):
        for n in range(2, 6):
            y_copy(i, n).wait()
        total = parts[i, y].astype(F32) + y_r2[i, 0].astype(F32) + y_r2[i, 1].astype(F32)
        gi_ref[pl.ds(i * C, C), :] = total.reshape(DB, C).astype(BF).T

    def c_copy(w):
        return remote(
            wg.at[w, :, :, 1 - c], c_r.at[w], c_s.at[w], c_rs.at[w], sib
        )

    def weight(w):
        cols = d_t[pl.ds(w * G, G), :]

        def block(i, carry):
            rows = pl.ds(pl.multiple_of(i * (D // NZ), D // NZ), D // NZ)
            value = nt(frt[rows, :], cols)
            wg[w, i] = value.astype(BF).reshape(NX, NC, R, G)
            return carry

        lax.fori_loop(0, NZ, block, 0)
        c_copy(w).start()

    x_next, x_prev, x_far = (lax.rem(x + d, NX) for d in (1, NX - 1, 2))

    def xw_copy(w, n):
        src, dst, dev = (
            (w_s1.at[w, x_far, 0], x_r1.at[w, 0], x_next),
            (w_s1.at[w, x_far, 1], x_r1.at[w, 1], x_prev),
            (w_s1.at[w, x_next, 1], x_r2.at[w, 0, 1], x_next),
            (w_s1.at[w, x_prev, 0], x_r2.at[w, 1, 0], x_prev),
            (w_s1.at[w, x_next, 0], x_r2.at[w, 0, 0], x_next),
            (w_s1.at[w, x_prev, 1], x_r2.at[w, 1, 1], x_prev),
        )[n]
        return remote(src, dst, w_s.at[w, n], w_r.at[w, n], at(z, dev, c))

    def w_core(w):
        c_copy(w).wait()
        for b in range(NX):
            value = wg[w, :, b, c].astype(F32) + c_r[w, :, b].astype(F32)
            w_s1[w, b] = value.astype(BF).reshape(2, NZ // 2, R, G)
        for n in range(4):
            xw_copy(w, n).start()

    def w_relay(w):
        for n, dest, half in ((0, x_next, 0), (1, x_prev, 1)):
            xw_copy(w, n).wait()
            w_s1[w, dest, half] = (
                w_s1[w, dest, half].astype(F32) + x_r1[w, half].astype(F32)
            ).astype(BF)
            xw_copy(w, 4 + n).start()

    def wz_copy(w, d):
        zt = lax.rem(z + d, NZ)
        return remote(
            w_s2.at[w, zt], z_r.at[w, d - 1], wz_s.at[w, d - 1], wz_r.at[w, d - 1],
            at(zt, x, c),
        )

    def w_cross(w):
        for n in range(2, 6):
            xw_copy(w, n).wait()
        value = w_s1[w, x].astype(F32) + x_r2[w, 0].astype(F32) + x_r2[w, 1].astype(F32)
        value = value.reshape(NZ, R, G)
        w_s2f[w] = value
        w_s2[w] = value.astype(BF)
        for d in range(1, NZ):
            wz_copy(w, d).start()

    def w_final(w, out):
        total = w_s2f[w, z]
        for d in range(1, NZ):
            wz_copy(w, d).wait()
            total = total + z_r[w, d - 1].astype(F32)
        out[...] = total

    finish(0)
    part(0)
    finish(1)
    part(1)
    y_relay(0)
    finish(2)
    finish(3)
    weight(0)
    weight(1)
    w_core(0)
    part(2)
    y_relay(1)
    weight(2)
    w_core(1)
    w_relay(0)
    part(3)
    y_relay(2)
    w_core(2)
    w_relay(1)
    w_cross(0)
    w_relay(2)
    y_relay(3)
    w_cross(1)
    y_final(0)
    w_cross(2)
    y_final(1)
    w_final(0, gwq_ref)
    w_final(1, gwk_ref)
    w_final(2, gwv_ref)
    y_final(2)
    y_final(3)


def build(mesh, interpret_dims=None):
    chunk, dh = interpret_dims or (CHUNK, DH)

    def local(frames, grad_out, w_query, w_key, w_value):
        T, D = frames.shape
        G = w_query.shape[1]
        NM, NY = mesh.shape["tm"], mesh.shape["head"]
        NZ = NM // (NX * NC)
        NH = G // dh
        C = chunk
        NCH = T // C
        R, DB = D // NM, D // NY
        HB = DB // 2
        dims = dict(T=T, D=D, G=G, C=C, NZ=NZ, NY=NY, NH=NH, DH=dh)
        V = pltpu.VMEM
        S = pltpu.SemaphoreType.DMA
        scratch = [
            V((T, D), BF), V((T, G), BF), V((D, 3 * G), BF), V((T, G), BF),
            V((G, T), BF), V((G, T), BF), V((G, T), BF), V((G, T), BF), V((D, T), BF),
            V((NCH, G, G), F32), V((NCH, G, G), F32),
            V((2, dh, G), F32), V((2, dh, G), BF),
            V((dh, G), BF), V((dh, G), BF), V((NZ - 1, dh, G), BF), V((dh, G), F32),
            V((2, dh, G), BF), V((NX - 1, dh, G), BF), V((dh, G), BF), V((dh, G), BF),
            V((2, dh, G), F32),
            V((3 * G, T), F32), V((3 * G, T), BF),
            V((NCH, NY, 2, HB, C), BF), V((NCH, 2, HB, C), BF), V((NCH, 2, 2, HB, C), BF),
            V((3, NZ, NX, NC, R, G), BF), V((3, NZ, NX, R, G), BF),
            V((3, NX, 2, NZ // 2, R, G), BF), V((3, 2, NZ // 2, R, G), BF),
            V((3, 2, 2, NZ // 2, R, G), BF),
            V((3, NZ, R, G), BF), V((3, NZ, R, G), F32), V((3, NZ - 1, R, G), BF),
            S((4 + NCH,)), S((2,)), S((2,)), S((NZ - 1,)), S((NZ - 1,)), S((NX - 1,)), S((NX - 1,)),
            S((NCH, 6)), S((NCH, 6)), S((3,)), S((3,)), S((3, 6)), S((3, 6)),
            S((3, NZ - 1)), S((3, NZ - 1)),
        ]
        anyspace = pl.BlockSpec(memory_space=pl.ANY)
        vm = pl.BlockSpec(memory_space=pltpu.VMEM)
        return pl.pallas_call(
            functools.partial(kernel, dims),
            out_shape=[
                jax.ShapeDtypeStruct((T, DB), BF),
                jax.ShapeDtypeStruct((R, G), F32),
                jax.ShapeDtypeStruct((R, G), F32),
                jax.ShapeDtypeStruct((R, G), F32),
            ],
            in_specs=[anyspace] * 5,
            out_specs=[vm] * 4,
            scratch_shapes=scratch,
            compiler_params=pltpu.CompilerParams(
                collective_id=0, has_side_effects=True, vmem_limit_bytes=48 * 2**20
            ),
        )(frames, grad_out, w_query, w_key, w_value)

    placed = (P("tm", None), P("tm", "head"), P(None, "head"), P(None, "head"), P(None, "head"))
    return jax.shard_map(
        local,
        mesh=mesh,
        in_specs=placed,
        out_specs=(P("tm", "head"), P("tm", "head"), P("tm", "head"), P("tm", "head")),
        check_vma=False,
    )


def solution(mesh):
    return build(mesh)
```

time: 474 us -> 61.6 us (0.13)
  waiting for transfers between devices: 329 us -> 0 us
  other arithmetic: 59.2 us -> 0 us
  matrix products: 57.6 us -> 0 us
  Pallas kernels: 0 us -> 52.3 us
  between operations: 13.9 us -> 0.65 us
    all_gather x2 -> x0, waiting for transfers between devices: 166 us -> none  [entering(): gathered = lax.all_gather(part, axis)]
    unnamed x5 -> x0, waiting for transfers between devices: 126 us -> none
    add x63 -> x0, other arithmetic: 59.2 us -> none  [add_states(): return earlier + later]
    dot_general x33 -> x0, matrix products: 57.6 us -> none  [the longest x9 23.5 us: contract_first(): lax.dot_general(left, right, (((0,), (0,)), ((), ())), preferred_element_...]
    pallas_call x0 -> x1, Pallas kernels: none -> 52.3 us  [local(): pl.pallas_call(functools.partial(kernel, dims), out_shape=[jax.ShapeDtype...]
    reduce_scatter x1 -> x0, waiting for transfers between devices: 37.5 us -> none  [local(): lax.psum_scatter(input_part.astype(jnp.bfloat16), 'head', scatter_dimensi...]
  transfers between devices with their start and end apart: 4 -> 0, of which waited for: 4 -> 0; matrix products, arithmetic and copies ran while one was open for 2% -> 0% of each run, Pallas kernels for 0% -> 0%
where the time goes in v1:
time: 61.6 us; the launch traced here: 61.3 us
  Pallas kernels  52.3 us (85%)
  local copies, waits for them, and re-layouts  8.36 us (14%)
  between operations  0.65 us (1%)
    pallas_call x1, Pallas kernels, local(): pl.pallas_call(functools.partial(kernel, dims), out_shape=[jax.ShapeDtype...  52.3 us
    unnamed x14, local copies, waits for them, and re-layouts  8.36 us

profile of v1, /device:TPU:1, one launch (start us, length us, event | category | flops | bytes accessed | tf_op | source)
XLA Modules:
  0.0 61.3 jit_solution(17566320648301550403)
XLA Ops:
  0.6 0.0 copy-start
  0.6 1.6 %copy-done = bf16[1024,1024]{1,0:T(8,128)(2,1)S(1)} copy-done((bf16[1024,1024]{1,0:T(8,128)(2,1)S(1)}, bf16[1024,1024]{1,0:T(8,128)(2,1)}, u32[]{:S(2)}) %copy-start) | copy-done | bytes 2097176
  2.2 0.0 copy-start.1
  2.2 1.0 %copy-done.1 = bf16[1024,256]{1,0:T(8,128)(2,1)S(1)} copy-done((bf16[1024,256]{1,0:T(8,128)(2,1)S(1)}, bf16[1024,256]{1,0:T(8,128)(2,1)}, u32[]{:S(2)}) %copy-start.1) | copy-done | bytes 524312
  3.3 0.0 copy-start.2
  3.3 1.0 %copy-done.2 = bf16[1024,256]{1,0:T(8,128)(2,1)S(1)} copy-done((bf16[1024,256]{1,0:T(8,128)(2,1)S(1)}, bf16[1024,256]{1,0:T(8,128)(2,1)}, u32[]{:S(2)}) %copy-start.2) | copy-done | bytes 524312
  4.3 0.0 copy-start.3
  4.3 1.0 %copy-done.3 = bf16[1024,256]{1,0:T(8,128)(2,1)S(1)} copy-done((bf16[1024,256]{1,0:T(8,128)(2,1)S(1)}, bf16[1024,256]{1,0:T(8,128)(2,1)}, u32[]{:S(2)}) %copy-start.3) | copy-done | bytes 524312
  5.4 0.0 copy-start.4
  5.4 1.0 %copy-done.4 = bf16[1024,256]{1,0:T(8,128)(2,1)S(1)} copy-done((bf16[1024,256]{1,0:T(8,128)(2,1)S(1)}, bf16[1024,256]{1,0:T(8,128)(2,1)}, u32[]{:S(2)}) %copy-start.4) | copy-done | bytes 524312
  6.4 52.3 %shard_map.84 = (bf16[1024,256]{1,0:T(8,128)(2,1)S(1)}, f32[16,256]{1,0:T(8,128)S(1)}, f32[16,256]{1,0:T(8,128)S(1)}, f32[16,256]{1,0:T(8,128)S(1)}) custom-call(bf16[1024,1024]{1,0:T(8,128)(2,1)S(1)} %copy-done, bf16[1024,256]{1,0:T(8,128)(2,1)S(1)} %copy-done.1, bf16[1024,256]{1,0:T(8,128)(2,1)S(1)} %copy-done.2, bf16[1024,256]{1,0:T(8,128)(2,1)S(1)} %copy-done.3, ...), custom_call_target="tpu_custom_call" | custom-call | tf_op jit(solution)/shard_map/pallas_call | solution.py:448
  58.7 0.8 %copy.13 = bf16[1024,256]{1,0:T(8,128)(2,1)} copy(bf16[1024,256]{1,0:T(8,128)(2,1)S(1)} %get-tuple-element.8) | data formatting | bytes 1048576
  59.5 0.6 copy.14
  60.1 0.6 copy.15
  60.7 0.6 copy.16
Async XLA Ops:
  0.6 1.6 %copy-start = (bf16[1024,1024]{1,0:T(8,128)(2,1)S(1)}, bf16[1024,1024]{1,0:T(8,128)(2,1)}, u32[]{:S(2)}) copy-start(bf16[1024,1024]{1,0:T(8,128)(2,1)} %frames_hbm.1) | copy-start | bytes 6291460
  2.2 1.0 %copy-start.1 = (bf16[1024,256]{1,0:T(8,128)(2,1)S(1)}, bf16[1024,256]{1,0:T(8,128)(2,1)}, u32[]{:S(2)}) copy-start(bf16[1024,256]{1,0:T(8,128)(2,1)} %grad_hbm.1) | copy-start | bytes 1572868
  3.3 1.0 %copy-start.2 = (bf16[1024,256]{1,0:T(8,128)(2,1)S(1)}, bf16[1024,256]{1,0:T(8,128)(2,1)}, u32[]{:S(2)}) copy-start(bf16[1024,256]{1,0:T(8,128)(2,1)} %wq_hbm.1) | copy-start | bytes 1572868
  4.3 1.0 %copy-start.3 = (bf16[1024,256]{1,0:T(8,128)(2,1)S(1)}, bf16[1024,256]{1,0:T(8,128)(2,1)}, u32[]{:S(2)}) copy-start(bf16[1024,256]{1,0:T(8,128)(2,1)} %wk_hbm.1) | copy-start | bytes 1572868
  5.4 1.0 %copy-start.4 = (bf16[1024,256]{1,0:T(8,128)(2,1)S(1)}, bf16[1024,256]{1,0:T(8,128)(2,1)}, u32[]{:S(2)}) copy-start(bf16[1024,256]{1,0:T(8,128)(2,1)} %wv_hbm.1) | copy-start | bytes 1572868

commit v2 on v1

--- a/solution.py
+++ b/solution.py
@@ -38,11 +38,10 @@
     frames_hbm, grad_hbm, wq_hbm, wk_hbm, wv_hbm,
     gi_ref, gwq_ref, gwk_ref, gwv_ref,
     fr, g_tok, w_all, q_tok, qt, kt, vt, gt, frt,
-    kvc, qgc, st, stb, sc_r1, sc_k, sc_zr, sc_acc, sc_p, sc_xr, sc_e, sc_r4, fin,
+    kvc, qgc, st, stb, sc_r1, sc_k, sc_zs, sc_zr, sc_acc, sc_p, sc_xr, sc_e, sc_r4, fin,
     d_in, d_t, parts, y_r1, y_r2,
-    wg, c_r, w_s1, x_r1, x_r2, w_s2, w_s2f, z_r,
-    in_sem, sc_s, sc_rs, zs_s, zs_r, xs_s, xs_r,
-    y_s, y_r, c_s, c_rs, w_s, w_r, wz_s, wz_r,
+    gi_buf, gw_buf, wg, c_r, w_s1, x_r1, x_r2, w_s2, w_s2f, z_r,
+    in_sem, out_sem, sc_s, sc_rs, zs_r, xs_r, y_s, y_r, c_rs, w_s, w_r, wz_r,
 ):
     T, D, G, C, NZ, NY, NH, dh = (
         dims[k] for k in ("T", "D", "G", "C", "NZ", "NY", "NH", "DH")
@@ -75,8 +74,8 @@
         for i, ref in enumerate((wq_hbm, wk_hbm, wv_hbm))
     ]
     copy_g = pltpu.make_async_copy(grad_hbm, g_tok, in_sem.at[3])
+    copies_in[0].start()
     copies_w[1].start()
-    copies_in[0].start()
     copies_w[2].start()
     copies_w[0].start()
     copy_g.start()
@@ -105,15 +104,16 @@
             total = total + full[h * dh : (h + 1) * dh]
         return total
 
-    copies_w[0].wait()
-    copies_w[1].wait()
-    copies_w[2].wait()
-    copy_g.wait()
-    for i in range(NCH):
-        copies_in[i].wait()
+    def wait_in():
+        for copy in copies_w:
+            copy.wait()
+        copy_g.wait()
+
+    wait_in()
 
     def project(i, carry):
         here = pl.ds(pl.multiple_of(i * C, C), C)
+        pltpu.make_async_copy(frames_hbm.at[here, :], fr.at[here, :], in_sem.at[4 + i]).wait()
         f = fr[here, :]
         k = nn(f, w_all[:, G : 2 * G]).astype(BF).T
         v = nn(f, w_all[:, 2 * G :]).astype(BF).T
@@ -142,6 +142,9 @@
             device_id=dev, device_id_type=MESH,
         )
 
+    def take(ref, sem):
+        pltpu.make_async_copy(ref, ref, sem).wait()
+
     scan1 = remote(stb.at[1 - c], sc_r1, sc_s.at[0], sc_rs.at[0], sib)
     scan1.start()
 
@@ -149,61 +152,87 @@
     zp = z + c * (NZ - 1 - 2 * z)
     xp = x + c * (NX - 1 - 2 * x)
 
-    def z_copy(d):
+    hd = dh // 2
+    far_first = sorted(range(1, NZ), key=lambda n: -min(n, NZ - n))
+
+    def z_copy(half, d):
         return remote(
-            sc_k, sc_zr.at[d - 1], zs_s.at[d - 1], zs_r.at[d - 1],
+            sc_zs.at[half], sc_zr.at[half, d - 1], sc_s.at[2], zs_r.at[half, d - 1],
             at(lax.rem(z + side * d + NZ, NZ), x, c),
         )
 
-    def scan_z_start():
-        scan1.wait()
-        sc_k[...] = (st[c] + sc_r1[...].astype(F32)).astype(BF)
-        for d in range(1, NZ):
+    def z_start(half):
+        for d in far_first:
             @pl.when(zp + d < NZ)
             def _():
-                z_copy(d).start()
-
-    def x_copy(d, src):
-        return remote(
-            src, sc_xr.at[d - 1], xs_s.at[d - 1], xs_r.at[d - 1],
-            at(z, lax.rem(x + d, NX), c),
-        )
-
-    def scan_x_start():
-        sc_acc[...] = jnp.zeros_like(sc_acc)
+                z_copy(half, d).start()
+
+    def z_gather(half):
+        rows = pl.ds(half * hd, hd)
         for d in range(1, NZ):
-            @pl.when(zp + d < NZ)
-            def _():
-                z_copy(d).wait_send()
-
             @pl.when(zp >= d)
             def _():
-                z_copy(d).wait_recv()
-                sc_acc[...] += sc_zr[d - 1].astype(F32)
-        own = sc_acc[...]
+                z_copy(half, d).wait_recv()
+                sc_acc[rows] += sc_zr[half, d - 1].astype(F32)
+
+    def x_copy(half, d, src):
+        return remote(
+            src, sc_xr.at[half, d - 1], sc_s.at[3], xs_r.at[half, d - 1],
+            at(z, lax.rem(x + d, NX), c),
+        )
+
+    def scan_start():
+        scan1.wait_recv()
+        chip = st[c] + sc_r1[...].astype(F32)
+        sc_k[...] = chip
+        sc_p[2] = chip[hd:].astype(BF)
+        sc_zs[0] = chip[:hd].astype(BF)
+        for d in range(1, NX):
+            x_copy(1, d, sc_p.at[2]).start()
+        z_start(0)
+        sc_acc[...] = jnp.zeros_like(sc_acc)
+
+    def scan_mid_b():
+        total = sc_k[pl.ds(hd, hd)]
+        ahead = jnp.zeros_like(total)
+        for d in range(1, NX):
+            x_copy(1, d, sc_p.at[2]).wait_recv()
+        for d in range(1, NX):
+            xs = lax.rem(x + NX - d, NX)
+            value = sc_xr[1, d - 1].astype(F32)
+            total = total + value
+            ahead = ahead + jnp.where(side * (x - xs) > 0, value, 0.0)
+        sc_acc[pl.ds(hd, hd)] = ahead
+        sc_zs[1] = total.astype(BF)
+        z_start(1)
+
+    def scan_mid_a():
+        z_gather(0)
+        own = sc_acc[pl.ds(0, hd)]
         sc_p[0] = own.astype(BF)
-        sc_p[1] = (own + st[c] + sc_r1[...].astype(F32)).astype(BF)
+        sc_p[1] = (own + sc_k[pl.ds(0, hd)]).astype(BF)
         for d in range(1, NX):
             xt = lax.rem(x + d, NX)
             later = jnp.where(side * (xt - x) > 0, 1, 0)
-            x_copy(d, sc_p.at[later]).start()
-
-    scan4 = remote(sc_e, sc_r4, sc_s.at[1], sc_rs.at[1], sib)
-
-    def scan_core_start():
+            x_copy(0, d, sc_p.at[later]).start()
+
+    def scan_fin():
         for d in range(1, NX):
-            xt = lax.rem(x + d, NX)
-            later = jnp.where(side * (xt - x) > 0, 1, 0)
-            x_copy(d, sc_p.at[later]).wait()
+            x_copy(0, d, sc_p.at[0]).wait_recv()
+        own = sc_acc[pl.ds(0, hd)]
+        for d in range(1, NX):
+            own = own + sc_xr[0, d - 1].astype(F32)
+        sc_acc[pl.ds(0, hd)] = own
+        z_gather(1)
         own = sc_acc[...]
-        for d in range(1, NX):
-            own = own + sc_xr[d - 1].astype(F32)
         fin[c] = own
         sc_e[...] = (own + st[c]).astype(BF)
         scan4.start()
 
+    scan4 = remote(sc_e, sc_r4, sc_s.at[1], sc_rs.at[1], sib)
+
     def scan_end():
-        scan4.wait()
+        scan4.wait_recv()
         fin[1 - c] = sc_r4[...].astype(F32)
 
     tri = lax.broadcasted_iota(jnp.int32, (C, C), 0) >= lax.broadcasted_iota(
@@ -233,16 +262,17 @@
             frt[pl.ds(b * C, C), here] = fr[here, pl.ds(b * C, C)].T
 
     intra(0)
-    scan_z_start()
+    scan_start()
     intra(1)
     flip(0)
+    flip(1)
     intra(2)
-    flip(1)
-    scan_x_start()
+    scan_mid_b()
     intra(3)
     flip(2)
-    scan_core_start()
     flip(3)
+    scan_mid_a()
+    scan_fin()
     scan_end()
 
     def finish(i):
@@ -266,20 +296,17 @@
     HB = DB // 2
 
     def part(i):
-        here = pl.ds(i * C, C)
-        grads = d_t[:, here]
-        for d in (2, 1, NY - 1, 0):
-            b = lax.rem(y + d, NY)
-            rows = pl.ds(pl.multiple_of(b * DB, DB), DB)
-            value = nn(w_all[rows, :], grads).astype(BF)
-            parts[i, b] = value.reshape(2, HB, C)
-            if d == 2:
-                y_copy(i, 0).start()
-                y_copy(i, 1).start()
-            if d == 1:
-                y_copy(i, 2).start()
-            if d == NY - 1:
-                y_copy(i, 3).start()
+        grads = d_t[:, pl.ds(i * C, C)]
+        for b in range(NY):
+            value = nn(w_all[pl.ds(b * DB, DB), :], grads).astype(BF)
+            parts[i, b, 0] = value[:HB]
+            parts[i, b, 1] = value[HB:]
+        for n in range(2):
+            y_copy(i, n).start()
+
+    def y_own(i):
+        for n in range(2, 4):
+            y_copy(i, n).start()
 
     def y_copy(i, n):
         src, dst, dev = (
@@ -290,37 +317,44 @@
             (parts.at[i, y_next, 0], y_r2.at[i, 0, 0], y_next),
             (parts.at[i, y_prev, 1], y_r2.at[i, 1, 1], y_prev),
         )[n]
-        return remote(src, dst, y_s.at[i, n], y_r.at[i, n], (me, dev))
+        return remote(src, dst, y_s.at[0], y_r.at[i, 0 if n < 2 else 1], (me, dev))
 
     def y_relay(i):
+        take(y_r1.at[i], y_r.at[i, 0])
         for n, dest, half in ((0, y_next, 0), (1, y_prev, 1)):
-            y_copy(i, n).wait()
             parts[i, dest, half] = (
                 parts[i, dest, half].astype(F32) + y_r1[i, half].astype(F32)
             ).astype(BF)
             y_copy(i, 4 + n).start()
 
     def y_final(i):
-        for n in range(2, 6):
-            y_copy(i, n).wait()
+        take(y_r2.at[i], y_r.at[i, 1])
         total = parts[i, y].astype(F32) + y_r2[i, 0].astype(F32) + y_r2[i, 1].astype(F32)
-        gi_ref[pl.ds(i * C, C), :] = total.reshape(DB, C).astype(BF).T
+        gi_buf[pl.ds(i * C, C), :] = total.reshape(DB, C).astype(BF).T
+        out_copy(i).start()
+
+    def out_copy(i):
+        rows = pl.ds(i * C, C)
+        return pltpu.make_async_copy(gi_buf.at[rows, :], gi_ref.at[rows, :], out_sem.at[0])
 
     def c_copy(w):
         return remote(
-            wg.at[w, :, :, 1 - c], c_r.at[w], c_s.at[w], c_rs.at[w], sib
+            wg.at[w, :, :, 1 - c], c_r.at[w], w_s.at[0], c_rs.at[w], sib
         )
 
     def weight(w):
         cols = d_t[pl.ds(w * G, G), :]
 
-        def block(i, carry):
-            rows = pl.ds(pl.multiple_of(i * (D // NZ), D // NZ), D // NZ)
-            value = nt(frt[rows, :], cols)
-            wg[w, i] = value.astype(BF).reshape(NX, NC, R, G)
-            return carry
-
-        lax.fori_loop(0, NZ, block, 0)
+        span = D // 4
+        per = NZ // 4 if NZ >= 4 else 0
+        for i in range(4):
+            value = nt(frt[pl.ds(i * span, span), :], cols).astype(BF)
+            if per:
+                wg[w, pl.ds(i * per, per)] = value.reshape(per, NX, NC, R, G)
+            else:
+                wg[w, i * NZ // 4, pl.ds((i % 2) * NX // 2, NX // 2)] = value.reshape(
+                    NX // 2, NC, R, G
+                )
         c_copy(w).start()
 
     x_next, x_prev, x_far = (lax.rem(x + d, NX) for d in (1, NX - 1, 2))
@@ -334,19 +368,25 @@
             (w_s1.at[w, x_next, 0], x_r2.at[w, 0, 0], x_next),
             (w_s1.at[w, x_prev, 1], x_r2.at[w, 1, 1], x_prev),
         )[n]
-        return remote(src, dst, w_s.at[w, n], w_r.at[w, n], at(z, dev, c))
+        return remote(
+            src, dst, w_s.at[1], w_r.at[w, 0 if n < 2 else 1], at(z, dev, c)
+        )
 
     def w_core(w):
-        c_copy(w).wait()
+        c_copy(w).wait_recv()
         for b in range(NX):
             value = wg[w, :, b, c].astype(F32) + c_r[w, :, b].astype(F32)
             w_s1[w, b] = value.astype(BF).reshape(2, NZ // 2, R, G)
-        for n in range(4):
+        for n in range(2):
             xw_copy(w, n).start()
 
+    def w_own(w):
+        for n in range(2, 4):
+            xw_copy(w, n).start()
+
     def w_relay(w):
+        take(x_r1.at[w], w_r.at[w, 0])
         for n, dest, half in ((0, x_next, 0), (1, x_prev, 1)):
-            xw_copy(w, n).wait()
             w_s1[w, dest, half] = (
                 w_s1[w, dest, half].astype(F32) + x_r1[w, half].astype(F32)
             ).astype(BF)
@@ -355,58 +395,101 @@
     def wz_copy(w, d):
         zt = lax.rem(z + d, NZ)
         return remote(
-            w_s2.at[w, zt], z_r.at[w, d - 1], wz_s.at[w, d - 1], wz_r.at[w, d - 1],
+            w_s2.at[w, zt], z_r.at[w, d - 1], w_s.at[2], wz_r.at[w],
             at(zt, x, c),
         )
 
     def w_cross(w):
-        for n in range(2, 6):
-            xw_copy(w, n).wait()
+        take(x_r2.at[w], w_r.at[w, 1])
         value = w_s1[w, x].astype(F32) + x_r2[w, 0].astype(F32) + x_r2[w, 1].astype(F32)
         value = value.reshape(NZ, R, G)
         w_s2f[w] = value
         w_s2[w] = value.astype(BF)
+        for d in sorted(range(1, NZ), key=lambda n: -min(n, NZ - n)):
+            wz_copy(w, d).start()
+
+    def w_final(w):
+        total = w_s2f[w, z]
+        take(z_r.at[w], wz_r.at[w])
         for d in range(1, NZ):
-            wz_copy(w, d).start()
-
-    def w_final(w, out):
-        total = w_s2f[w, z]
-        for d in range(1, NZ):
-            wz_copy(w, d).wait()
             total = total + z_r[w, d - 1].astype(F32)
-        out[...] = total
+        gw_buf[w] = total
+        gw_copy(w).start()
+
+    def gw_copy(w):
+        return pltpu.make_async_copy(
+            gw_buf.at[w], (gwq_ref, gwk_ref, gwv_ref)[w], out_sem.at[0]
+        )
+
+    def y_drain():
+        for i in range(NCH):
+            out_copy(i).wait()
+        for w in range(3):
+            gw_copy(w).wait()
+        scan1.wait_send()
+        scan4.wait_send()
+        for half in range(2):
+            for d in range(1, NZ):
+                @pl.when(zp + d < NZ)
+                def _():
+                    z_copy(half, d).wait_send()
+            for d in range(1, NX):
+                x_copy(half, d, sc_p.at[0]).wait_send()
+        take(parts.at[:, pl.ds(0, 3)], y_s.at[0])
+        take(c_r, w_s.at[0])
+        take(w_s1.at[:, pl.ds(0, 3)], w_s.at[1])
+        take(z_r, w_s.at[2])
 
     finish(0)
     part(0)
+    y_own(0)
     finish(1)
-    part(1)
-    y_relay(0)
     finish(2)
     finish(3)
     weight(0)
+    part(1)
     weight(1)
     w_core(0)
+    y_own(1)
+    weight(2)
     part(2)
+    w_core(1)
+    w_own(0)
+    y_relay(0)
+    part(3)
+    y_own(2)
+    w_core(2)
+    w_own(1)
+    w_relay(0)
+    w_own(2)
+    w_relay(1)
     y_relay(1)
-    weight(2)
-    w_core(1)
-    w_relay(0)
-    part(3)
+    y_own(3)
+    w_relay(2)
     y_relay(2)
-    w_core(2)
-    w_relay(1)
     w_cross(0)
-    w_relay(2)
+    w_cross(1)
     y_relay(3)
-    w_cross(1)
+    w_cross(2)
     y_final(0)
-    w_cross(2)
     y_final(1)
-    w_final(0, gwq_ref)
-    w_final(1, gwk_ref)
-    w_final(2, gwv_ref)
+    w_final(0)
+    w_final(1)
     y_final(2)
+    w_final(2)
     y_final(3)
+    y_drain()
+
+
+def hand_over(a, b, c, d, oa, ob, oc, od, sem):
+    copies = [
+        pltpu.make_async_copy(src, dst, sem.at[n])
+        for n, (src, dst) in enumerate(((a, oa), (b, ob), (c, oc), (d, od)))
+    ]
+    for copy in copies:
+        copy.start()
+    for copy in copies:
+        copy.wait()
 
 
 def build(mesh, interpret_dims=None):
@@ -430,36 +513,51 @@
             V((G, T), BF), V((G, T), BF), V((G, T), BF), V((G, T), BF), V((D, T), BF),
             V((NCH, G, G), F32), V((NCH, G, G), F32),
             V((2, dh, G), F32), V((2, dh, G), BF),
-            V((dh, G), BF), V((dh, G), BF), V((NZ - 1, dh, G), BF), V((dh, G), F32),
-            V((2, dh, G), BF), V((NX - 1, dh, G), BF), V((dh, G), BF), V((dh, G), BF),
+            V((dh, G), BF), V((dh, G), F32), V((2, dh // 2, G), BF),
+            V((2, NZ - 1, dh // 2, G), BF), V((dh, G), F32),
+            V((3, dh // 2, G), BF), V((2, NX - 1, dh // 2, G), BF), V((dh, G), BF), V((dh, G), BF),
             V((2, dh, G), F32),
             V((3 * G, T), F32), V((3 * G, T), BF),
             V((NCH, NY, 2, HB, C), BF), V((NCH, 2, HB, C), BF), V((NCH, 2, 2, HB, C), BF),
+            V((T, DB), BF), V((3, R, G), F32),
             V((3, NZ, NX, NC, R, G), BF), V((3, NZ, NX, R, G), BF),
             V((3, NX, 2, NZ // 2, R, G), BF), V((3, 2, NZ // 2, R, G), BF),
             V((3, 2, 2, NZ // 2, R, G), BF),
             V((3, NZ, R, G), BF), V((3, NZ, R, G), F32), V((3, NZ - 1, R, G), BF),
-            S((4 + NCH,)), S((2,)), S((2,)), S((NZ - 1,)), S((NZ - 1,)), S((NX - 1,)), S((NX - 1,)),
-            S((NCH, 6)), S((NCH, 6)), S((3,)), S((3,)), S((3, 6)), S((3, 6)),
-            S((3, NZ - 1)), S((3, NZ - 1)),
+            S((4 + NCH,)), S((1,)), S((4,)), S((2,)), S((2, NZ - 1)), S((2, NX - 1)),
+            S((1,)), S((NCH, 2)), S((3,)), S((3,)), S((3, 2)), S((3,)),
         ]
         anyspace = pl.BlockSpec(memory_space=pl.ANY)
-        vm = pl.BlockSpec(memory_space=pltpu.VMEM)
-        return pl.pallas_call(
+        hbm = pl.BlockSpec(memory_space=pltpu.HBM)
+        shapes = [
+            jax.ShapeDtypeStruct((T, DB), BF),
+            jax.ShapeDtypeStruct((R, G), F32),
+            jax.ShapeDtypeStruct((R, G), F32),
+            jax.ShapeDtypeStruct((R, G), F32),
+        ]
+        results = pl.pallas_call(
             functools.partial(kernel, dims),
-            out_shape=[
-                jax.ShapeDtypeStruct((T, DB), BF),
-                jax.ShapeDtypeStruct((R, G), F32),
-                jax.ShapeDtypeStruct((R, G), F32),
-                jax.ShapeDtypeStruct((R, G), F32),
-            ],
-            in_specs=[anyspace] * 5,
-            out_specs=[vm] * 4,
+            out_shape=shapes,
+            in_specs=[hbm] * 5,
+            out_specs=[anyspace] * 4,
             scratch_shapes=scratch,
             compiler_params=pltpu.CompilerParams(
                 collective_id=0, has_side_effects=True, vmem_limit_bytes=48 * 2**20
             ),
-        )(frames, grad_out, w_query, w_key, w_value)
+        )(
+            *[
+                pltpu.with_memory_space_constraint(array, pltpu.HBM)
+                for array in (frames, grad_out, w_query, w_key, w_value)
+            ]
+        )
+        return pl.pallas_call(
+            hand_over,
+            out_shape=shapes,
+            in_specs=[anyspace] * 4,
+            out_specs=[hbm] * 4,
+            scratch_shapes=[S((4,))],
+            compiler_params=pltpu.CompilerParams(vmem_limit_bytes=4 * 2**20),
+        )(*results)
 
     placed = (P("tm", None), P("tm", "head"), P(None, "head"), P(None, "head"), P(None, "head"))
     return jax.shard_map(

time: 61.6 us -> 44 us (0.71)
  Pallas kernels: 52.3 us -> 43.2 us
  local copies, waits for them, and re-layouts: 8.36 us -> 0 us
    pallas_call x1 -> x2, Pallas kernels: 52.3 us -> 43.2 us  [the longest x1 42.4 us: local(): pl.pallas_call(functools.partial(kernel, dims), out_shape=shapes, in_spec...]
    unnamed x14 -> x0, local copies, waits for them, and re-layouts: 8.36 us -> none
where the time goes in v2:
time: 44 us; the launch traced here: 43.9 us
  Pallas kernels  43.2 us (98%)
  between operations  0.64 us (1%)
    pallas_call x1, Pallas kernels, local(): pl.pallas_call(functools.partial(kernel, dims), out_shape=shapes, in_spec...  42.4 us

profile of v2, /device:TPU:1, one launch (start us, length us, event | category | flops | bytes accessed | tf_op | source)
XLA Modules:
  0.0 43.9 jit_solution(8615816579822518267)
XLA Ops:
  0.6 42.4 %shard_map.84 = (bf16[1024,256]{1,0:T(8,128)(2,1)S(1)}, f32[16,256]{1,0:T(8,128)S(1)}, f32[16,256]{1,0:T(8,128)S(1)}, f32[16,256]{1,0:T(8,128)S(1)}) custom-call(bf16[1024,1024]{1,0:T(8,128)(2,1)} %frames_hbm.1, bf16[1024,256]{1,0:T(8,128)(2,1)} %grad_hbm.1, bf16[1024,256]{1,0:T(8,128)(2,1)} %wq_hbm.1, bf16[1024,256]{1,0:T(8,128)(2,1)} %wk_hbm.1, ...), custom_call_target="tpu_custom_call" | custom-call | tf_op jit(solution)/shard_map/pallas_call | solution.py:538
  43.0 0.8 %shard_map.85 = (bf16[1024,256]{1,0:T(8,128)(2,1)}, f32[16,256]{1,0:T(8,128)}, f32[16,256]{1,0:T(8,128)}, f32[16,256]{1,0:T(8,128)}) custom-call(bf16[1024,256]{1,0:T(8,128)(2,1)S(1)} %get-tuple-element.8.a, f32[16,256]{1,0:T(8,128)S(1)} %get-tuple-element.9.b, f32[16,256]{1,0:T(8,128)S(1)} %get-tuple-element.10.c, f32[16,256]{1,0:T(8,128)S(1)} %get-tuple-element.11.d), custom_call_target="tpu_custom_call" | custom-call | tf_op jit(solution)/shard_map/pallas_call | solution.py:553

commit v3 on v2

--- a/solution.py
+++ b/solution.py
@@ -28,16 +28,11 @@
     return lax.dot_general(a, b, (((0,), (0,)), ((), ())), preferred_element_type=F32)
 
 
-def split(value):
-    high = value.astype(BF)
-    return high, (value - high.astype(F32)).astype(BF)
-
-
 def kernel(
     dims,
     frames_hbm, grad_hbm, wq_hbm, wk_hbm, wv_hbm,
     gi_ref, gwq_ref, gwk_ref, gwv_ref,
-    fr, g_tok, w_all, q_tok, qt, kt, vt, gt, frt,
+    fr, g_tok, w_all, q_tok, k_tok, v_tok, kt, vt, gt, frt,
     kvc, qgc, st, stb, sc_r1, sc_k, sc_zs, sc_zr, sc_acc, sc_p, sc_xr, sc_e, sc_r4, fin,
     d_in, d_t, parts, y_r1, y_r2,
     gi_buf, gw_buf, wg, c_r, w_s1, x_r1, x_r2, w_s2, w_s2f, z_r,
@@ -74,13 +69,11 @@
         for i, ref in enumerate((wq_hbm, wk_hbm, wv_hbm))
     ]
     copy_g = pltpu.make_async_copy(grad_hbm, g_tok, in_sem.at[3])
-    copies_in[0].start()
-    copies_w[1].start()
-    copies_w[2].start()
-    copies_w[0].start()
+    for copy in copies_w:
+        copy.start()
+    for copy in copies_in:
+        copy.start()
     copy_g.start()
-    for i in range(1, NCH):
-        copies_in[i].start()
 
     barrier = pltpu.get_barrier_semaphore()
     peers = [sib]
@@ -104,32 +97,36 @@
             total = total + full[h * dh : (h + 1) * dh]
         return total
 
-    def wait_in():
+    def chunk(i):
+        return pl.ds(i * C, C)
+
+    def project_one(w, out, i):
+        out[chunk(i), :] = nn(fr[chunk(i), :], w_all[:, w * G : (w + 1) * G]).astype(BF)
+
+    def state_one(left, right, out, i):
+        out[i] = jnp.where(same, tn(left[chunk(i), :], right[chunk(i), :]), 0.0)
+
+    def project_first():
         for copy in copies_w:
             copy.wait()
+        copies_in[0].wait()
+        project_one(1, k_tok, 0)
+        project_one(2, v_tok, 0)
+        project_one(0, q_tok, 0)
+
+    def project_rest():
+        for copy in copies_in[1:]:
+            copy.wait()
         copy_g.wait()
-
-    wait_in()
-
-    def project(i, carry):
-        here = pl.ds(pl.multiple_of(i * C, C), C)
-        pltpu.make_async_copy(frames_hbm.at[here, :], fr.at[here, :], in_sem.at[4 + i]).wait()
-        f = fr[here, :]
-        k = nn(f, w_all[:, G : 2 * G]).astype(BF).T
-        v = nn(f, w_all[:, 2 * G :]).astype(BF).T
-        kt[:, here] = k
-        vt[:, here] = v
-        kvc[i] = jnp.where(same, nt(k, v), 0.0)
-        q = nn(f, w_all[:, :G]).astype(BF)
-        q_tok[here, :] = q
-        qf = q.T
-        qt[:, here] = qf
-        g = g_tok[here, :]
-        gt[:, here] = g.T
-        qgc[i] = jnp.where(same, nn(qf, g), 0.0)
-        return carry
-
-    lax.fori_loop(0, NCH, project, 0)
+        for w, out in ((1, k_tok), (2, v_tok), (0, q_tok)):
+            for i in range(1, NCH):
+                project_one(w, out, i)
+        for i in range(NCH):
+            state_one(k_tok, v_tok, kvc, i)
+            state_one(q_tok, g_tok, qgc, i)
+
+    project_first()
+    project_rest()
 
     st[0] = pack(sum(kvc[i] for i in range(NCH)))
     st[1] = pack(sum(qgc[i] for i in range(NCH)))
@@ -154,6 +151,8 @@
 
     hd = dh // 2
     far_first = sorted(range(1, NZ), key=lambda n: -min(n, NZ - n))
+
+    x_far_first = sorted(range(1, NX), key=lambda n: -min(n, NX - n))
 
     def z_copy(half, d):
         return remote(
@@ -187,7 +186,7 @@
         sc_k[...] = chip
         sc_p[2] = chip[hd:].astype(BF)
         sc_zs[0] = chip[:hd].astype(BF)
-        for d in range(1, NX):
+        for d in x_far_first:
             x_copy(1, d, sc_p.at[2]).start()
         z_start(0)
         sc_acc[...] = jnp.zeros_like(sc_acc)
@@ -211,7 +210,7 @@
         own = sc_acc[pl.ds(0, hd)]
         sc_p[0] = own.astype(BF)
         sc_p[1] = (own + sc_k[pl.ds(0, hd)]).astype(BF)
-        for d in range(1, NX):
+        for d in x_far_first:
             xt = lax.rem(x + d, NX)
             later = jnp.where(side * (xt - x) > 0, 1, 0)
             x_copy(0, d, sc_p.at[later]).start()
@@ -244,7 +243,13 @@
         here = pl.ds(i * C, C)
         g = g_tok[here, :]
         q = q_tok[here, :]
-        kf, vf, qf, gf = kt[:, here], vt[:, here], qt[:, here], gt[:, here]
+        qf = q.T
+        gf = g.T
+        kf = k_tok[here, :].T
+        vf = v_tok[here, :].T
+        gt[:, here] = gf
+        kt[:, here] = kf
+        vt[:, here] = vf
         zero = jnp.zeros_like(g)
         for h in range(NH):
             rows = slice(h * dh, (h + 1) * dh)
@@ -261,17 +266,17 @@
         for b in range(D // C):
             frt[pl.ds(b * C, C), here] = fr[here, pl.ds(b * C, C)].T
 
-    intra(0)
-    scan_start()
-    intra(1)
     flip(0)
     flip(1)
+    scan_start()
+    intra(0)
+    intra(1)
+    scan_mid_b()
     intra(2)
-    scan_mid_b()
+    flip(2)
+    scan_mid_a()
     intra(3)
-    flip(2)
     flip(3)
-    scan_mid_a()
     scan_fin()
     scan_end()
 
@@ -283,12 +288,12 @@
             prefix = prefix + kvc[j]
         for j in range(i + 1, NCH):
             suffix = suffix + qgc[j]
-        ph, pe = split(prefix)
-        sh, se = split(suffix)
+        prefix = prefix.astype(BF)
+        suffix = suffix.astype(BF)
         kf, vf, gf = kt[:, here], vt[:, here], gt[:, here]
-        dq = d_in[pl.ds(0, G), here] + nn(ph, gf) + nn(pe, gf)
-        dk = d_in[pl.ds(G, G), here] + nn(sh, vf) + nn(se, vf)
-        dv = d_in[pl.ds(2 * G, G), here] + tn(sh, kf) + tn(se, kf)
+        dq = d_in[pl.ds(0, G), here] + nn(prefix, gf)
+        dk = d_in[pl.ds(G, G), here] + nn(suffix, vf)
+        dv = d_in[pl.ds(2 * G, G), here] + tn(suffix, kf)
         d_t[pl.ds(0, G), here] = (dq * scale).astype(BF)
         d_t[pl.ds(G, G), here] = (dk * scale).astype(BF)
         d_t[pl.ds(2 * G, G), here] = (dv * scale).astype(BF)
@@ -297,6 +302,20 @@
 
     def part(i):
         grads = d_t[:, pl.ds(i * C, C)]
+        if i == 0:
+            rows = pl.ds(pl.multiple_of(y_far * DB, DB), DB)
+            value = nn(w_all[rows, :], grads).astype(BF)
+            parts[i, y_far, 0] = value[:HB]
+            parts[i, y_far, 1] = value[HB:]
+            y_copy(i, 0).start()
+            y_copy(i, 1).start()
+            for d in (1, NY - 1, 0):
+                b = lax.rem(y + d, NY)
+                rows = pl.ds(pl.multiple_of(b * DB, DB), DB)
+                value = nn(w_all[rows, :], grads).astype(BF)
+                parts[i, b, 0] = value[:HB]
+                parts[i, b, 1] = value[HB:]
+            return
         for b in range(NY):
             value = nn(w_all[pl.ds(b * DB, DB), :], grads).astype(BF)
             parts[i, b, 0] = value[:HB]
@@ -448,29 +467,29 @@
     finish(3)
     weight(0)
     part(1)
+    y_own(1)
     weight(1)
+    weight(2)
     w_core(0)
-    y_own(1)
-    weight(2)
+    w_own(0)
+    y_relay(0)
     part(2)
     w_core(1)
-    w_own(0)
-    y_relay(0)
     part(3)
     y_own(2)
     w_core(2)
     w_own(1)
     w_relay(0)
     w_own(2)
-    w_relay(1)
     y_relay(1)
     y_own(3)
+    w_relay(1)
     w_relay(2)
-    y_relay(2)
     w_cross(0)
     w_cross(1)
+    y_relay(2)
+    w_cross(2)
     y_relay(3)
-    w_cross(2)
     y_final(0)
     y_final(1)
     w_final(0)
@@ -484,8 +503,12 @@
 def hand_over(a, b, c, d, oa, ob, oc, od, sem):
     copies = [
         pltpu.make_async_copy(src, dst, sem.at[n])
-        for n, (src, dst) in enumerate(((a, oa), (b, ob), (c, oc), (d, od)))
+        for n, (src, dst) in enumerate(((b, ob), (c, oc), (d, od)))
     ]
+    step = a.shape[0] // 4
+    for n in range(4):
+        rows = pl.ds(n * step, step)
+        copies.append(pltpu.make_async_copy(a.at[rows, :], oa.at[rows, :], sem.at[3 + n]))
     for copy in copies:
         copy.start()
     for copy in copies:
@@ -509,8 +532,9 @@
         V = pltpu.VMEM
         S = pltpu.SemaphoreType.DMA
         scratch = [
-            V((T, D), BF), V((T, G), BF), V((D, 3 * G), BF), V((T, G), BF),
-            V((G, T), BF), V((G, T), BF), V((G, T), BF), V((G, T), BF), V((D, T), BF),
+            V((T, D), BF), V((T, G), BF), V((D, 3 * G), BF),
+            V((T, G), BF), V((T, G), BF), V((T, G), BF),
+            V((G, T), BF), V((G, T), BF), V((G, T), BF), V((D, T), BF),
             V((NCH, G, G), F32), V((NCH, G, G), F32),
             V((2, dh, G), F32), V((2, dh, G), BF),
             V((dh, G), BF), V((dh, G), F32), V((2, dh // 2, G), BF),
@@ -555,7 +579,7 @@
             out_shape=shapes,
             in_specs=[anyspace] * 4,
             out_specs=[hbm] * 4,
-            scratch_shapes=[S((4,))],
+            scratch_shapes=[S((7,))],
             compiler_params=pltpu.CompilerParams(vmem_limit_bytes=4 * 2**20),
         )(*results)
 

time: 44 us -> 42.4 us (0.964)
  Pallas kernels: 43.2 us -> 41.6 us
    pallas_call x1, Pallas kernels: 42.4 us -> 40.8 us  [local(): pl.pallas_call(functools.partial(kernel, dims), out_shape=shapes, in_spec...]
where the time goes in v3:
time: 42.4 us; the launch traced here: 42.3 us
  Pallas kernels  41.6 us (98%)
  between operations  0.64 us (2%)
    pallas_call x1, Pallas kernels, local(): pl.pallas_call(functools.partial(kernel, dims), out_shape=shapes, in_spec...  40.8 us
    pallas_call x1, Pallas kernels, local(): pl.pallas_call(hand_over, out_shape=shapes, in_specs=[anyspace] * 4, out_...  0.86 us

profile of v3, /device:TPU:1, one launch (start us, length us, event | category | flops | bytes accessed | tf_op | source)
XLA Modules:
  0.0 42.3 jit_solution(5540798150394910297)
XLA Ops:
  0.6 40.8 %shard_map.84 = (bf16[1024,256]{1,0:T(8,128)(2,1)S(1)}, f32[16,256]{1,0:T(8,128)S(1)}, f32[16,256]{1,0:T(8,128)S(1)}, f32[16,256]{1,0:T(8,128)S(1)}) custom-call(bf16[1024,1024]{1,0:T(8,128)(2,1)} %frames_hbm.1, bf16[1024,256]{1,0:T(8,128)(2,1)} %grad_hbm.1, bf16[1024,256]{1,0:T(8,128)(2,1)} %wq_hbm.1, bf16[1024,256]{1,0:T(8,128)(2,1)} %wk_hbm.1, ...), custom_call_target="tpu_custom_call" | custom-call | tf_op jit(solution)/shard_map/pallas_call | solution.py:562
  41.4 0.9 %shard_map.85 = (bf16[1024,256]{1,0:T(8,128)(2,1)}, f32[16,256]{1,0:T(8,128)}, f32[16,256]{1,0:T(8,128)}, f32[16,256]{1,0:T(8,128)}) custom-call(bf16[1024,256]{1,0:T(8,128)(2,1)S(1)} %get-tuple-element.8.a, f32[16,256]{1,0:T(8,128)S(1)} %get-tuple-element.9.b, f32[16,256]{1,0:T(8,128)S(1)} %get-tuple-element.10.c, f32[16,256]{1,0:T(8,128)S(1)} %get-tuple-element.11.d), custom_call_target="tpu_custom_call" | custom-call | tf_op jit(solution)/shard_map/pallas_call | solution.py:577

commit v4 on v3

--- a/solution.py
+++ b/solution.py
@@ -267,15 +267,15 @@
             frt[pl.ds(b * C, C), here] = fr[here, pl.ds(b * C, C)].T
 
     flip(0)
-    flip(1)
     scan_start()
     intra(0)
     intra(1)
     scan_mid_b()
+    scan_mid_a()
     intra(2)
+    intra(3)
+    flip(1)
     flip(2)
-    scan_mid_a()
-    intra(3)
     flip(3)
     scan_fin()
     scan_end()

time: 42.4 us -> 41.8 us (0.986)
  Pallas kernels: 41.6 us -> 41.1 us
    pallas_call x1, Pallas kernels: 40.8 us -> 40.2 us  [local(): pl.pallas_call(functools.partial(kernel, dims), out_shape=shapes, in_spec...]
where the time goes in v4:
time: 41.8 us; the launch traced here: 41.7 us
  Pallas kernels  41.1 us (98%)
  between operations  0.64 us (2%)
    pallas_call x1, Pallas kernels, local(): pl.pallas_call(functools.partial(kernel, dims), out_shape=shapes, in_spec...  40.2 us
    pallas_call x1, Pallas kernels, local(): pl.pallas_call(hand_over, out_shape=shapes, in_specs=[anyspace] * 4, out_...  0.86 us

profile of v4, /device:TPU:1, one launch (start us, length us, event | category | flops | bytes accessed | tf_op | source)
XLA Modules:
  0.0 41.7 jit_solution(10409275771023765922)
XLA Ops:
  0.6 40.2 %shard_map.84 = (bf16[1024,256]{1,0:T(8,128)(2,1)S(1)}, f32[16,256]{1,0:T(8,128)S(1)}, f32[16,256]{1,0:T(8,128)S(1)}, f32[16,256]{1,0:T(8,128)S(1)}) custom-call(bf16[1024,1024]{1,0:T(8,128)(2,1)} %frames_hbm.1, bf16[1024,256]{1,0:T(8,128)(2,1)} %grad_hbm.1, bf16[1024,256]{1,0:T(8,128)(2,1)} %wq_hbm.1, bf16[1024,256]{1,0:T(8,128)(2,1)} %wk_hbm.1, ...), custom_call_target="tpu_custom_call" | custom-call | tf_op jit(solution)/shard_map/pallas_call | solution.py:562
  40.9 0.9 %shard_map.85 = (bf16[1024,256]{1,0:T(8,128)(2,1)}, f32[16,256]{1,0:T(8,128)}, f32[16,256]{1,0:T(8,128)}, f32[16,256]{1,0:T(8,128)}) custom-call(bf16[1024,256]{1,0:T(8,128)(2,1)S(1)} %get-tuple-element.8.a, f32[16,256]{1,0:T(8,128)S(1)} %get-tuple-element.9.b, f32[16,256]{1,0:T(8,128)S(1)} %get-tuple-element.10.c, f32[16,256]{1,0:T(8,128)S(1)} %get-tuple-element.11.d), custom_call_target="tpu_custom_call" | custom-call | tf_op jit(solution)/shard_map/pallas_call | solution.py:577

commit v5 on v4

--- a/solution.py
+++ b/solution.py
@@ -176,7 +176,7 @@
 
     def x_copy(half, d, src):
         return remote(
-            src, sc_xr.at[half, d - 1], sc_s.at[3], xs_r.at[half, d - 1],
+            src, sc_xr.at[half, d - 1], sc_s.at[3], xs_r.at[half],
             at(z, lax.rem(x + d, NX), c),
         )
 
@@ -194,8 +194,7 @@
     def scan_mid_b():
         total = sc_k[pl.ds(hd, hd)]
         ahead = jnp.zeros_like(total)
-        for d in range(1, NX):
-            x_copy(1, d, sc_p.at[2]).wait_recv()
+        take(sc_xr.at[1], xs_r.at[1])
         for d in range(1, NX):
             xs = lax.rem(x + NX - d, NX)
             value = sc_xr[1, d - 1].astype(F32)
@@ -216,8 +215,7 @@
             x_copy(0, d, sc_p.at[later]).start()
 
     def scan_fin():
-        for d in range(1, NX):
-            x_copy(0, d, sc_p.at[0]).wait_recv()
+        take(sc_xr.at[0], xs_r.at[0])
         own = sc_acc[pl.ds(0, hd)]
         for d in range(1, NX):
             own = own + sc_xr[0, d - 1].astype(F32)
@@ -452,8 +450,7 @@
                 @pl.when(zp + d < NZ)
                 def _():
                     z_copy(half, d).wait_send()
-            for d in range(1, NX):
-                x_copy(half, d, sc_p.at[0]).wait_send()
+            take(sc_xr.at[half], sc_s.at[3])
         take(parts.at[:, pl.ds(0, 3)], y_s.at[0])
         take(c_r, w_s.at[0])
         take(w_s1.at[:, pl.ds(0, 3)], w_s.at[1])
@@ -548,7 +545,7 @@
             V((3, NX, 2, NZ // 2, R, G), BF), V((3, 2, NZ // 2, R, G), BF),
             V((3, 2, 2, NZ // 2, R, G), BF),
             V((3, NZ, R, G), BF), V((3, NZ, R, G), F32), V((3, NZ - 1, R, G), BF),
-            S((4 + NCH,)), S((1,)), S((4,)), S((2,)), S((2, NZ - 1)), S((2, NX - 1)),
+            S((4 + NCH,)), S((1,)), S((4,)), S((2,)), S((2, NZ - 1)), S((2,)),
             S((1,)), S((NCH, 2)), S((3,)), S((3,)), S((3, 2)), S((3,)),
         ]
         anyspace = pl.BlockSpec(memory_space=pl.ANY)

time: 41.8 us -> 41.8 us (level)
  no operation moved by 1% of the time
where the time goes in v5:
time: 41.8 us; the launch traced here: 41.7 us
  Pallas kernels  41.1 us (98%)
  between operations  0.64 us (2%)
    pallas_call x1, Pallas kernels, local(): pl.pallas_call(functools.partial(kernel, dims), out_shape=shapes, in_spec...  40.2 us
    pallas_call x1, Pallas kernels, local(): pl.pallas_call(hand_over, out_shape=shapes, in_specs=[anyspace] * 4, out_...  0.86 us

profile of v5, /device:TPU:1, one launch (start us, length us, event | category | flops | bytes accessed | tf_op | source)
XLA Modules:
  0.0 41.7 jit_solution(13544169743264795658)
XLA Ops:
  0.6 40.2 %shard_map.84 = (bf16[1024,256]{1,0:T(8,128)(2,1)S(1)}, f32[16,256]{1,0:T(8,128)S(1)}, f32[16,256]{1,0:T(8,128)S(1)}, f32[16,256]{1,0:T(8,128)S(1)}) custom-call(bf16[1024,1024]{1,0:T(8,128)(2,1)} %frames_hbm.1, bf16[1024,256]{1,0:T(8,128)(2,1)} %grad_hbm.1, bf16[1024,256]{1,0:T(8,128)(2,1)} %wq_hbm.1, bf16[1024,256]{1,0:T(8,128)(2,1)} %wk_hbm.1, ...), custom_call_target="tpu_custom_call" | custom-call | tf_op jit(solution)/shard_map/pallas_call | solution.py:559
  40.8 0.9 %shard_map.85 = (bf16[1024,256]{1,0:T(8,128)(2,1)}, f32[16,256]{1,0:T(8,128)}, f32[16,256]{1,0:T(8,128)}, f32[16,256]{1,0:T(8,128)}) custom-call(bf16[1024,256]{1,0:T(8,128)(2,1)S(1)} %get-tuple-element.8.a, f32[16,256]{1,0:T(8,128)S(1)} %get-tuple-element.9.b, f32[16,256]{1,0:T(8,128)S(1)} %get-tuple-element.10.c, f32[16,256]{1,0:T(8,128)S(1)} %get-tuple-element.11.d), custom_call_target="tpu_custom_call" | custom-call | tf_op jit(solution)/shard_map/pallas_call | solution.py:574
